TPU v7x, 32 devices: a whole 2x2x4 slice. The times are simulated.
32 devices in a mesh: prefix: 16 (over z, x, core), tensor: 2 (over y).
Axes of the slice: x: 2, y: 2, z: 4, core: 2. Of those that a mesh axis runs over, the one named last changes fastest.
Arguments:
- queries: bfloat16 [1024, 8192], P(('prefix', 'tensor')), may hold values from -24 to 24
- suffix_kv: bfloat16 [1024, 2, 8, 64, 128], P('prefix', None, 'tensor'), may hold values from -15 to 15
- suffix_lengths: int32 [1024], P('prefix'), may hold values from 1 to 64
- prefix_kv: bfloat16 [16, 2, 8, 4096, 128], P('prefix', None, 'tensor'), may hold values from -16 to 16
- tree_ids: int32 [1024], P('prefix'), may hold values from 0 to 15, as said below
- owner_map: int32 [16], replicated, may hold values from 0 to 15, as said below
Outputs:
- attended: bfloat16 [1024, 8192], P(('prefix', 'tensor'))
Inputs may be any that keep to these rules, and one draw needn't show every extreme that they name: `tree_ids`: in each aligned block of 64 rows (the rows of one index of prefix) no prompt is named by more than 8 rows, and some prompt is named by exactly 8 rows in every block. `owner_map`: A permutation: every row of prefix_kv holds the prefix of exactly one prompt.
All inputs are finite; a program needn't handle non-finite values.
Results may differ from a plain program's by a relative error of at most 0.0017.
Values may be sent and summed in bfloat16 or wider, within the bound.
A program may use at most 64 MiB of HBM per device.

v0:
```python
import math

import jax
import jax.numpy as jnp
from jax import lax
from jax.sharding import PartitionSpec as P

H = 64
KVH = 8
HD = 128


def prefix_attend(slot_block, key_rows, value_rows):
    sources, slot_count, row_width = slot_block.shape
    kv_heads = key_rows.shape[0]
    group_size = row_width // (kv_heads * HD)
    per_source = slot_count * (row_width // HD)
    pieces = math.gcd(sources, max(1, sources * per_source // 512))
    shaped = slot_block.reshape(pieces, sources // pieces, slot_count, kv_heads, group_size, HD)
    score_scale = 1.0 / math.sqrt(HD)

    def attend_piece(query_piece):
        scores = (
            jnp.einsum(
                "skgid,gnd->skgin", query_piece, key_rows, preferred_element_type=jnp.float32
            )
            * score_scale
        )
        row_top = jnp.max(scores, axis=-1)
        weights = jnp.exp(scores - row_top[..., None])
        mass_sum = jnp.sum(weights, axis=-1)
        weighted = jnp.einsum(
            "skgin,gnd->skgid",
            weights.astype(jnp.bfloat16),
            value_rows,
            preferred_element_type=jnp.float32,
        )
        return (weighted / mass_sum[..., None], row_top, mass_sum)

    prefix_part, prefix_top, prefix_total = lax.map(attend_piece, shaped)
    head_count = row_width // HD
    return (
        prefix_part.reshape(sources, slot_count, row_width),
        prefix_top.reshape(sources, slot_count, head_count),
        prefix_total.reshape(sources, slot_count, head_count),
    )


def on_device(queries, suffix_kv, suffix_lengths, prefix_kv, tree_ids, owner_map):
    owners = lax.axis_size("prefix")
    head_groups = lax.axis_size("tensor")
    kv_local = KVH // head_groups
    group_size = H // KVH
    row_width = H // head_groups * HD
    score_scale = 1.0 / math.sqrt(HD)
    local_q = lax.all_to_all(queries, "tensor", split_axis=1, concat_axis=0, tiled=True)
    rows_home = local_q.shape[0]
    capacity = max(2, 2 * rows_home // owners)
    prompts = owner_map.shape[0]
    prompt_iota = jnp.arange(prompts, dtype=jnp.int32)
    prompt_match = tree_ids[:, None] == prompt_iota[None, :]
    owner_row = jnp.sum(jnp.where(prompt_match, owner_map[None, :], 0), axis=1)
    row_iota = jnp.arange(rows_home, dtype=jnp.int32)
    earlier = (tree_ids[:, None] == tree_ids[None, :]) & (row_iota[None, :] < row_iota[:, None])
    slot_rank = jnp.sum(earlier.astype(jnp.int32), axis=1)
    owner_iota = jnp.arange(owners, dtype=jnp.int32)
    slot_iota = jnp.arange(capacity, dtype=jnp.int32)
    placed = (owner_row[None, None, :] == owner_iota[:, None, None]) & (
        slot_rank[None, None, :] == slot_iota[None, :, None]
    )
    key_rows = prefix_kv[0, 0]
    value_rows = prefix_kv[0, 1]
    outgoing = jnp.einsum(
        "ojr,rc->ojc", placed.astype(jnp.bfloat16), local_q, preferred_element_type=jnp.float32
    ).astype(jnp.bfloat16)
    part_slots, top_slots, total_slots = prefix_attend(
        lax.all_to_all(outgoing, "prefix", split_axis=0, concat_axis=0, tiled=True),
        key_rows,
        value_rows,
    )
    returned = (
        lax.all_to_all(part_slots, "prefix", split_axis=0, concat_axis=0, tiled=True),
        lax.all_to_all(top_slots, "prefix", split_axis=0, concat_axis=0, tiled=True),
        lax.all_to_all(total_slots, "prefix", split_axis=0, concat_axis=0, tiled=True),
    )
    back_part, back_top, back_total = returned
    picker = placed.astype(jnp.float32)
    prefix_part = jnp.einsum("ojr,ojc->rc", picker, back_part, precision=lax.Precision.HIGHEST)
    prefix_top = jnp.einsum("ojr,ojh->rh", picker, back_top, precision=lax.Precision.HIGHEST)
    prefix_total = jnp.einsum("ojr,ojh->rh", picker, back_total, precision=lax.Precision.HIGHEST)
    prefix_part = prefix_part.reshape(rows_home, kv_local, group_size, HD)
    prefix_top = prefix_top.reshape(rows_home, kv_local, group_size)
    prefix_total = prefix_total.reshape(rows_home, kv_local, group_size)
    query_home = local_q.reshape(rows_home, kv_local, group_size, HD)
    suffix_scores = (
        jnp.einsum(
            "rgid,rgnd->rgin", query_home, suffix_kv[:, 0], preferred_element_type=jnp.float32
        )
        * score_scale
    )
    position = jnp.arange(suffix_kv.shape[3], dtype=jnp.int32)
    is_live = (position[None, :] < suffix_lengths[:, None])[:, None, None, :]
    suffix_top = jnp.max(jnp.where(is_live, suffix_scores, -jnp.inf), axis=-1)
    suffix_weights = jnp.where(is_live, jnp.exp(suffix_scores - suffix_top[..., None]), 0.0)
    suffix_total = jnp.sum(suffix_weights, axis=-1)
    suffix_sum = jnp.einsum(
        "rgin,rgnd->rgid",
        suffix_weights.astype(jnp.bfloat16),
        suffix_kv[:, 1],
        preferred_element_type=jnp.float32,
    )
    joint_top = jnp.maximum(prefix_top, suffix_top)
    prefix_mass = prefix_total * jnp.exp(prefix_top - joint_top)
    suffix_mass = jnp.exp(suffix_top - joint_top)
    attended = (prefix_mass[..., None] * prefix_part + suffix_mass[..., None] * suffix_sum) / (
        prefix_mass + suffix_mass * suffix_total
    )[..., None]
    attended = attended.reshape(rows_home, row_width).astype(jnp.bfloat16)
    return lax.all_to_all(attended, "tensor", split_axis=0, concat_axis=1, tiled=True)


def solution(mesh):
    in_specs = (
        P(("prefix", "tensor"), None),
        P("prefix", None, "tensor", None, None),
        P("prefix"),
        P("prefix", None, "tensor", None, None),
        P("prefix"),
        P(),
    )
    out_specs = P(("prefix", "tensor"), None)
    return jax.shard_map(
        on_device, mesh=mesh, in_specs=in_specs, out_specs=out_specs, check_vma=False
    )
```

profile of v0, /device:TPU:10, one launch (start us, length us, event | category | flops | bytes accessed | tf_op | source)
XLA Modules:
  0.0 201.1 jit_solution(10913667716007548081)
XLA Ops:
  0.0 1.9 copy.104
  1.9 3.5 %all-to-all-start = ((bf16[32,2,4096]{2,0,1:T(8,128)(2,1)}), bf16[32,2,4096]{2,0,1:T(8,128)(2,1)S(1)}, u32[]{:S(2)}, u32[]{:S(2)}) async-start(bf16[32,2,4096]{2,0,1:T(8,128)(2,1)} %bitcast.109), calls=%async_computation | async-start | bytes 1048576 | tf_op jit(solution)/shard_map/all_to_all | solution.py:56
  7.1 6.5 %all-to-all-done = bf16[32,2,4096]{2,0,1:T(8,128)(2,1)S(1)} async-done(((bf16[32,2,4096]{2,0,1:T(8,128)(2,1)}), bf16[32,2,4096]{2,0,1:T(8,128)(2,1)S(1)}, u32[]{:S(2)}, u32[]{:S(2)}) %all-to-all-start) | async-done | bytes 524320 | tf_op jit(solution)/shard_map/all_to_all | solution.py:56
  15.0 6.2 %all-to-all-start.1 = ((bf16[16,8,4096]{2,1,0:T(8,128)(2,1)}), bf16[16,8,4096]{2,1,0:T(8,128)(2,1)S(1)}, u32[]{:S(2)}, u32[]{:S(2)}) async-start(bf16[16,8,4096]{2,1,0:T(8,128)(2,1)} %convolution_convert_fusion), calls=%async_computation.1 | async-start | bytes 2097152 | tf_op jit(solution)/shard_map/all_to_all | solution.py:77
  21.3 5.7 %slice_bitcast_fusion = (bf16[4,4096,128]{2,1,0:T(8,128)(2,1)}, bf16[4,4096,128]{2,1,0:T(8,128)(2,1)}) fusion(bf16[1,2,4,4096,128]{4,3,2,1,0:T(8,128)(2,1)} %param.11), kind=kLoop, calls=%fused_computation.27 | loop fusion | bytes 16777216 | tf_op jit(solution)/shard_map/squeeze | solution.py:72
  27.0 18.8 %all-to-all-done.1 = bf16[16,8,4096]{2,1,0:T(8,128)(2,1)S(1)} async-done(((bf16[16,8,4096]{2,1,0:T(8,128)(2,1)}), bf16[16,8,4096]{2,1,0:T(8,128)(2,1)S(1)}, u32[]{:S(2)}, u32[]{:S(2)}) %all-to-all-start.1) | async-done | bytes 1048608 | tf_op jit(solution)/shard_map/all_to_all | solution.py:77
  45.8 65.1 %while.14 = (s32[]{:T(128)}, f32[8,2,8,4,8,128]{5,2,4,3,1,0:T(8,128)}, f32[8,2,8,4,8]{4,3,2,1,0:T(4,128)S(1)}, f32[8,2,8,4,8]{4,3,2,1,0:T(4,128)S(1)}, bf16[8,2,...) while((s32[]{:T(128)}, ...), condition=%wide.region_5.6_spmd, body=%wide.region_2.5_spmd.sunk | while | flops 1090583552 | bytes 51652740 | solution.py:40
  45.8 3.5 %bitcast_reduce_fusion.2 = (f32[2,8,4,8]{3,1,0,2:T(8,128)S(1)}, f32[4,2,8,8,4096]{4,3,2,1,0:T(8,128)S(1)}) fusion(bf16[4,4096,128]{2,1,0:T(8,128)(2,1)} %get-tuple-element.172, bf16[1,2,8,4,8,128]{5,2,4,3,1,0:T(8,128)(2,1)S(1)} %constant_dynamic-slice_fusion.2), kind=kOutput, calls=%fused_computation.1.clone.1 | convolution fusion | flops 541064704 | bytes 12716032 | tf_op jit(solution)/shard_map/while/body/eval_jaxpr/skgid,gnd->skgin/dot_general | solution.py:24
  51.5 1.6 fusion.81
  54.0 3.5 %bitcast_reduce_fusion.2 = (f32[2,8,4,8]{3,1,0,2:T(8,128)S(1)}, f32[4,2,8,8,4096]{4,3,2,1,0:T(8,128)S(1)}) fusion(bf16[4,4096,128]{2,1,0:T(8,128)(2,1)} %get-tuple-element.172, bf16[1,2,8,4,8,128]{5,2,4,3,1,0:T(8,128)(2,1)S(1)} %constant_dynamic-slice_fusion.2), kind=kOutput, calls=%fused_computation.1.clone.1 | convolution fusion | flops 541064704 | bytes 12716032 | tf_op jit(solution)/shard_map/while/body/eval_jaxpr/skgid,gnd->skgin/dot_general | solution.py:24
  59.7 1.6 fusion.81
  62.1 3.5 %bitcast_reduce_fusion.2 = (f32[2,8,4,8]{3,1,0,2:T(8,128)S(1)}, f32[4,2,8,8,4096]{4,3,2,1,0:T(8,128)S(1)}) fusion(bf16[4,4096,128]{2,1,0:T(8,128)(2,1)} %get-tuple-element.172, bf16[1,2,8,4,8,128]{5,2,4,3,1,0:T(8,128)(2,1)S(1)} %constant_dynamic-slice_fusion.2), kind=kOutput, calls=%fused_computation.1.clone.1 | convolution fusion | flops 541064704 | bytes 12716032 | tf_op jit(solution)/shard_map/while/body/eval_jaxpr/skgid,gnd->skgin/dot_general | solution.py:24
  67.8 1.6 fusion.81
  70.2 3.5 %bitcast_reduce_fusion.2 = (f32[2,8,4,8]{3,1,0,2:T(8,128)S(1)}, f32[4,2,8,8,4096]{4,3,2,1,0:T(8,128)S(1)}) fusion(bf16[4,4096,128]{2,1,0:T(8,128)(2,1)} %get-tuple-element.172, bf16[1,2,8,4,8,128]{5,2,4,3,1,0:T(8,128)(2,1)S(1)} %constant_dynamic-slice_fusion.2), kind=kOutput, calls=%fused_computation.1.clone.1 | convolution fusion | flops 541064704 | bytes 12716032 | tf_op jit(solution)/shard_map/while/body/eval_jaxpr/skgid,gnd->skgin/dot_general | solution.py:24
  76.0 1.6 fusion.81
  78.4 3.5 %bitcast_reduce_fusion.2 = (f32[2,8,4,8]{3,1,0,2:T(8,128)S(1)}, f32[4,2,8,8,4096]{4,3,2,1,0:T(8,128)S(1)}) fusion(bf16[4,4096,128]{2,1,0:T(8,128)(2,1)} %get-tuple-element.172, bf16[1,2,8,4,8,128]{5,2,4,3,1,0:T(8,128)(2,1)S(1)} %constant_dynamic-slice_fusion.2), kind=kOutput, calls=%fused_computation.1.clone.1 | convolution fusion | flops 541064704 | bytes 12716032 | tf_op jit(solution)/shard_map/while/body/eval_jaxpr/skgid,gnd->skgin/dot_general | solution.py:24
  84.1 1.6 fusion.81
  86.5 3.5 %bitcast_reduce_fusion.2 = (f32[2,8,4,8]{3,1,0,2:T(8,128)S(1)}, f32[4,2,8,8,4096]{4,3,2,1,0:T(8,128)S(1)}) fusion(bf16[4,4096,128]{2,1,0:T(8,128)(2,1)} %get-tuple-element.172, bf16[1,2,8,4,8,128]{5,2,4,3,1,0:T(8,128)(2,1)S(1)} %constant_dynamic-slice_fusion.2), kind=kOutput, calls=%fused_computation.1.clone.1 | convolution fusion | flops 541064704 | bytes 12716032 | tf_op jit(solution)/shard_map/while/body/eval_jaxpr/skgid,gnd->skgin/dot_general | solution.py:24
  92.3 1.6 fusion.81
  94.7 3.5 %bitcast_reduce_fusion.2 = (f32[2,8,4,8]{3,1,0,2:T(8,128)S(1)}, f32[4,2,8,8,4096]{4,3,2,1,0:T(8,128)S(1)}) fusion(bf16[4,4096,128]{2,1,0:T(8,128)(2,1)} %get-tuple-element.172, bf16[1,2,8,4,8,128]{5,2,4,3,1,0:T(8,128)(2,1)S(1)} %constant_dynamic-slice_fusion.2), kind=kOutput, calls=%fused_computation.1.clone.1 | convolution fusion | flops 541064704 | bytes 12716032 | tf_op jit(solution)/shard_map/while/body/eval_jaxpr/skgid,gnd->skgin/dot_general | solution.py:24
  100.4 1.6 fusion.81
  102.8 3.5 %bitcast_reduce_fusion.2 = (f32[2,8,4,8]{3,1,0,2:T(8,128)S(1)}, f32[4,2,8,8,4096]{4,3,2,1,0:T(8,128)S(1)}) fusion(bf16[4,4096,128]{2,1,0:T(8,128)(2,1)} %get-tuple-element.172, bf16[1,2,8,4,8,128]{5,2,4,3,1,0:T(8,128)(2,1)S(1)} %constant_dynamic-slice_fusion.2), kind=kOutput, calls=%fused_computation.1.clone.1 | convolution fusion | flops 541064704 | bytes 12716032 | tf_op jit(solution)/shard_map/while/body/eval_jaxpr/skgid,gnd->skgin/dot_general | solution.py:24
  108.6 1.6 fusion.81
  111.8 5.1 %all-to-all-start.3 = ((f32[16,1,256]{2,1,0:T(1,128)}), f32[16,1,256]{2,1,0:T(1,128)S(1)}, u32[]{:S(2)}, u32[]{:S(2)}) async-start(f32[16,1,256]{2,1,0:T(1,128)} %reshape.157), calls=%async_computation.3 | async-start | bytes 32768 | tf_op jit(solution)/shard_map/all_to_all | solution.py:83
  117.2 3.9 %all-to-all-done.3 = f32[16,1,256]{2,1,0:T(1,128)S(1)} async-done(((f32[16,1,256]{2,1,0:T(1,128)}), f32[16,1,256]{2,1,0:T(1,128)S(1)}, u32[]{:S(2)}, u32[]{:S(2)}) %all-to-all-start.3) | async-done | bytes 16416 | tf_op jit(solution)/shard_map/all_to_all | solution.py:83
  121.1 9.1 %all_to_all.55 = f32[16,1,256]{2,1,0:T(1,128)S(1)} all-to-all(f32[16,1,256]{2,1,0:T(1,128)S(1)} %reshape.155), channel_id=1, replica_groups=mesh['prefix'=16,'tensor'=2] {'prefix'}, dimensions={0} | all-to-all | bytes 32768 | tf_op jit(solution)/shard_map/all_to_all | solution.py:84
  130.2 6.0 %all-to-all-start.4 = ((f32[16,8,4096]{2,1,0:T(8,128)}), f32[16,8,4096]{2,1,0:T(8,128)S(1)}, u32[]{:S(2)}, u32[]{:S(2)}) async-start(f32[16,8,4096]{2,1,0:T(8,128)} %bitcast.136), calls=%async_computation.4 | async-start | bytes 4194304 | tf_op jit(solution)/shard_map/all_to_all | solution.py:82
  136.3 4.6 %select_reduce_fusion = (f32[64,4,8]{2,1,0:T(4,128)S(1)}, f32[64,4,8,64]{3,2,1,0:T(8,128)S(1)}) fusion(pred[64,64]{1,0:T(8,128)(4,1)S(1)} %iota_compare_fusion, bf16[64,4,8,128]{3,2,1,0:T(8,128)(2,1)S(1)} %bitcast.135, bf16[64,2,4,64,128]{4,3,2,1,0:T(8,128)(2,1)} %param.9), kind=kOutput, calls=%fused_computation.40 | convolution fusion | flops 33945600 | bytes 5255168 | tf_op jit(solution)/shard_map/rgid,rgnd->rgin/dot_general | solution.py:96
  147.4 35.9 %all-to-all-done.4 = f32[16,8,4096]{2,1,0:T(8,128)S(1)} async-done(((f32[16,8,4096]{2,1,0:T(8,128)}), f32[16,8,4096]{2,1,0:T(8,128)S(1)}, u32[]{:S(2)}, u32[]{:S(2)}) %all-to-all-start.4) | async-done | bytes 2097184 | tf_op jit(solution)/shard_map/all_to_all | solution.py:82
  183.3 2.1 %fusion.34 = f32[8,8,32,128]{3,1,2,0:T(8,128)S(1)} fusion(f32[16,8,4096]{2,1,0:T(8,128)S(1)} %all-to-all-done.4, pred[8,64]{1,0:T(8,128)(4,1)S(1)} %iota_compare_fusion.4, pred[16,64]{1,0:T(8,128)(4,1)S(1)} %iota_compare_fusion.2), kind=kOutput, calls=%fused_computation.31 | convolution fusion | flops 402661376 | bytes 3147264 | tf_op jit(solution)/shard_map/ojr,ojc->rc/dot_general | solution.py:88
  185.7 3.1 %divide_convert_fusion = bf16[64,4,8,128]{3,2,1,0:T(8,128)(2,1)S(1)} fusion(bf16[64,2,4,64,128]{4,3,2,1,0:T(8,128)(2,1)} %param.9, f32[64,4,8,128]{3,2,1,0:T(8,128)S(1)} %bitcast.138, f32[64,4,8,64]{3,2,1,0:T(8,128)S(1)} %get-tuple-element.98, f32[64,4,8]{2,1,0:T(4,128)S(1)} %copy.66, f32[64,4,8]{2,1,0:T(4,128)S(1)} %get-tuple-element.97, ...), kind=kOutput, calls=%fused_computation.38 | convolution fusion | flops 35258368 | bytes 6328320 | tf_op jit(solution)/shard_map/rgin,rgnd->rgid/dot_general | solution.py:106
  189.0 11.2 %all_to_all.56 = bf16[2,32,4096]{2,1,0:T(8,128)(2,1)S(1)} all-to-all(bf16[2,32,4096]{2,1,0:T(8,128)(2,1)S(1)} %convert_element_type.25), channel_id=1, replica_groups=mesh['prefix'=16,'tensor'=2] {'tensor'}, dimensions={0} | all-to-all | bytes 1048576 | tf_op jit(solution)/shard_map/all_to_all | solution.py:119
  (83 shorter events, 36.1 us)
Async XLA Ops:
  1.9 11.7 %all-to-all-start = ((bf16[32,2,4096]{2,0,1:T(8,128)(2,1)}), bf16[32,2,4096]{2,0,1:T(8,128)(2,1)S(1)}, u32[]{:S(2)}, u32[]{:S(2)}) async-start(bf16[32,2,4096]{2,0,1:T(8,128)(2,1)} %bitcast.109), calls=%async_computation | async-start | bytes 1048576 | tf_op jit(solution)/shard_map/all_to_all | solution.py:56
  15.0 30.8 %all-to-all-start.1 = ((bf16[16,8,4096]{2,1,0:T(8,128)(2,1)}), bf16[16,8,4096]{2,1,0:T(8,128)(2,1)S(1)}, u32[]{:S(2)}, u32[]{:S(2)}) async-start(bf16[16,8,4096]{2,1,0:T(8,128)(2,1)} %convolution_convert_fusion), calls=%async_computation.1 | async-start | bytes 2097152 | tf_op jit(solution)/shard_map/all_to_all | solution.py:77
  49.4 2.2 %copy-start = (bf16[4,4096,128]{2,1,0:T(8,128)(2,1)S(1)}, bf16[4,4096,128]{2,1,0:T(8,128)(2,1)}, u32[]{:S(2)}) copy-start(bf16[4,4096,128]{2,1,0:T(8,128)(2,1)} %get-tuple-element.173) | copy-start | bytes 12582916 | tf_op jit(solution)/shard_map/while
  57.5 2.2 %copy-start = (bf16[4,4096,128]{2,1,0:T(8,128)(2,1)S(1)}, bf16[4,4096,128]{2,1,0:T(8,128)(2,1)}, u32[]{:S(2)}) copy-start(bf16[4,4096,128]{2,1,0:T(8,128)(2,1)} %get-tuple-element.173) | copy-start | bytes 12582916 | tf_op jit(solution)/shard_map/while
  65.6 2.2 %copy-start = (bf16[4,4096,128]{2,1,0:T(8,128)(2,1)S(1)}, bf16[4,4096,128]{2,1,0:T(8,128)(2,1)}, u32[]{:S(2)}) copy-start(bf16[4,4096,128]{2,1,0:T(8,128)(2,1)} %get-tuple-element.173) | copy-start | bytes 12582916 | tf_op jit(solution)/shard_map/while
  73.8 2.2 %copy-start = (bf16[4,4096,128]{2,1,0:T(8,128)(2,1)S(1)}, bf16[4,4096,128]{2,1,0:T(8,128)(2,1)}, u32[]{:S(2)}) copy-start(bf16[4,4096,128]{2,1,0:T(8,128)(2,1)} %get-tuple-element.173) | copy-start | bytes 12582916 | tf_op jit(solution)/shard_map/while
  81.9 2.2 %copy-start = (bf16[4,4096,128]{2,1,0:T(8,128)(2,1)S(1)}, bf16[4,4096,128]{2,1,0:T(8,128)(2,1)}, u32[]{:S(2)}) copy-start(bf16[4,4096,128]{2,1,0:T(8,128)(2,1)} %get-tuple-element.173) | copy-start | bytes 12582916 | tf_op jit(solution)/shard_map/while
  90.1 2.2 %copy-start = (bf16[4,4096,128]{2,1,0:T(8,128)(2,1)S(1)}, bf16[4,4096,128]{2,1,0:T(8,128)(2,1)}, u32[]{:S(2)}) copy-start(bf16[4,4096,128]{2,1,0:T(8,128)(2,1)} %get-tuple-element.173) | copy-start | bytes 12582916 | tf_op jit(solution)/shard_map/while
  98.2 2.2 %copy-start = (bf16[4,4096,128]{2,1,0:T(8,128)(2,1)S(1)}, bf16[4,4096,128]{2,1,0:T(8,128)(2,1)}, u32[]{:S(2)}) copy-start(bf16[4,4096,128]{2,1,0:T(8,128)(2,1)} %get-tuple-element.173) | copy-start | bytes 12582916 | tf_op jit(solution)/shard_map/while
  106.4 2.2 %copy-start = (bf16[4,4096,128]{2,1,0:T(8,128)(2,1)S(1)}, bf16[4,4096,128]{2,1,0:T(8,128)(2,1)}, u32[]{:S(2)}) copy-start(bf16[4,4096,128]{2,1,0:T(8,128)(2,1)} %get-tuple-element.173) | copy-start | bytes 12582916 | tf_op jit(solution)/shard_map/while
  111.0 25.2 %copy-start.2 = (s32[64]{0:T(128)S(1)}, s32[64]{0:T(128)}, u32[]{:S(2)}) copy-start(s32[64]{0:T(128)} %param.10) | copy-start | bytes 772
  111.8 9.3 %all-to-all-start.3 = ((f32[16,1,256]{2,1,0:T(1,128)}), f32[16,1,256]{2,1,0:T(1,128)S(1)}, u32[]{:S(2)}, u32[]{:S(2)}) async-start(f32[16,1,256]{2,1,0:T(1,128)} %reshape.157), calls=%async_computation.3 | async-start | bytes 32768 | tf_op jit(solution)/shard_map/all_to_all | solution.py:83
  130.2 53.2 %all-to-all-start.4 = ((f32[16,8,4096]{2,1,0:T(8,128)}), f32[16,8,4096]{2,1,0:T(8,128)S(1)}, u32[]{:S(2)}, u32[]{:S(2)}) async-start(f32[16,8,4096]{2,1,0:T(8,128)} %bitcast.136), calls=%async_computation.4 | async-start | bytes 4194304 | tf_op jit(solution)/shard_map/all_to_all | solution.py:82
  183.3 2.3 %copy-start.1 = (f32[64,4,8]{2,1,0:T(4,128)S(1)}, f32[64,4,8]{2,1,0:T(4,128)}, u32[]{:S(2)}) copy-start(f32[64,4,8]{2,1,0:T(4,128)} %copy.59) | copy-start | bytes 24580
where the time goes:
time: 202 us; the launch traced here: 201 us
  waiting for transfers between devices  65.1 us (32%)
  matrix products  53.1 us (26%)
  local copies, waits for them, and re-layouts  25.3 us (13%)
  starting transfers between devices  20.8 us (10%)
  blocking collectives  20.3 us (10%)
  other arithmetic  15.9 us (8%)
    all_to_all x1, waiting for transfers between devices, on_device(): lax.all_to_all(part_slots, 'prefix', split_axis=0, concat_axis=0, tiled=T...  35.9 us
    dot_general x8, matrix products, attend_piece(): jnp.einsum('skgid,gnd->skgin', query_piece, key_rows, preferred_element_t...  28.2 us
    all_to_all x1, waiting for transfers between devices, on_device(): lax.all_to_all(outgoing, 'prefix', split_axis=0, concat_axis=0, tiled=True)  18.8 us
    dot_general x8, matrix products, attend_piece(): jnp.einsum('skgin,gnd->skgid', weights.astype(jnp.bfloat16), value_rows,...  12.7 us
    reduce_sum x8, other arithmetic, attend_piece(): mass_sum = jnp.sum(weights, axis=-1)  11.9 us
    all_to_all x1, blocking collectives, on_device(): lax.all_to_all(attended, 'tensor', split_axis=0, concat_axis=1, tiled=True)  11.2 us
    all_to_all x1, blocking collectives, on_device(): lax.all_to_all(total_slots, 'prefix', split_axis=0, concat_axis=0, tiled=...  9.05 us
    all_to_all x1, waiting for transfers between devices, on_device(): lax.all_to_all(queries, 'tensor', split_axis=1, concat_axis=0, tiled=True)  6.52 us
  transfers between devices with their start and end apart: 4, of which 4 were waited for; matrix products, arithmetic and copies ran while one was open for 9% of the time, Pallas kernels for 0%

commit v1 on v0

v1 whole, which is shorter than its diff:
```python
import math

import jax
import jax.numpy as jnp
from jax import lax
from jax.experimental import pallas as pl
from jax.experimental.pallas import tpu as pltpu
from jax.sharding import PartitionSpec as P

H = 64
KVH = 8
HD = 128
LANES = 128
GROUP = H // KVH
LOG2E = 1.4426950408889634
SCALE2 = LOG2E / math.sqrt(HD)


def nt_dot(a, b):
    return lax.dot_general(a, b, (((1,), (1,)), ((), ())), preferred_element_type=jnp.float32)


def nn_dot(a, b):
    return lax.dot_general(a, b, (((1,), (0,)), ((), ())), preferred_element_type=jnp.float32)


def prefix_kernel(q_ref, kv_ref, out_ref, lse_ref):
    g = pl.program_id(0)
    slots = q_ref.shape[0]
    length = kv_ref.shape[3]
    chunk = min(1024, length)
    pair = 2
    lane = lax.broadcasted_iota(jnp.int32, (slots, LANES), 1)

    @pl.when(g == 0)
    def _():
        lse_ref[...] = jnp.zeros_like(lse_ref)

    def one_tile(t, carry):
        cols = [pl.ds(pl.multiple_of((t * pair + i) * HD, HD), HD) for i in range(pair)]
        q = jnp.concatenate([q_ref[:, c] for c in cols], axis=0)
        top = total = acc = None
        for start in range(0, length, chunk):
            s = nt_dot(q, kv_ref[0, 0, 0, start : start + chunk, :]) * SCALE2
            here = jnp.max(s, axis=1, keepdims=True)
            new_top = here if top is None else jnp.maximum(top, here)
            w = jnp.exp2(s - new_top)
            w_sum = jnp.sum(w, axis=1, keepdims=True)
            w_v = nn_dot(w.astype(jnp.bfloat16), kv_ref[0, 1, 0, start : start + chunk, :])
            if top is None:
                total, acc = w_sum, w_v
            else:
                fade = jnp.exp2(top - new_top)
                total = total * fade + w_sum
                acc = acc * fade + w_v
            top = new_top
        part = (acc / total).astype(jnp.bfloat16)
        lse = top + jnp.log(total) * LOG2E
        for i in range(pair):
            rows = slice(i * slots, (i + 1) * slots)
            out_ref[:, cols[i]] = part[rows]
            head = g * GROUP + t * pair + i
            lse_ref[...] = jnp.where(lane == head, lse[rows], lse_ref[...])
        return carry

    lax.fori_loop(0, GROUP // pair, one_tile, 0)


def prefix_attend(slot_rows, prefix_kv):
    slots, row_width = slot_rows.shape
    kv_heads, length = prefix_kv.shape[2], prefix_kv.shape[3]
    wide = GROUP * HD
    return pl.pallas_call(
        prefix_kernel,
        grid=(kv_heads,),
        out_shape=(
            jax.ShapeDtypeStruct((slots, row_width), jnp.bfloat16),
            jax.ShapeDtypeStruct((slots, LANES), jnp.float32),
        ),
        in_specs=[
            pl.BlockSpec((slots, wide), lambda g: (0, g)),
            pl.BlockSpec((1, 2, 1, length, HD), lambda g: (0, 0, g, 0, 0)),
        ],
        out_specs=(
            pl.BlockSpec((slots, wide), lambda g: (0, g)),
            pl.BlockSpec((slots, LANES), lambda g: (0, 0)),
        ),
        compiler_params=pltpu.CompilerParams(vmem_limit_bytes=40 << 20),
        cost_estimate=pl.CostEstimate(
            flops=4 * slots * row_width * length,
            bytes_accessed=4 * kv_heads * length * HD + 4 * slots * row_width,
            transcendentals=slots * row_width // HD * length,
        ),
        name="prefix_attend",
    )(slot_rows, prefix_kv)


def suffix_kernel(q_ref, kv_ref, len_ref, sum_ref, lse_ref):
    rows, kv_heads, count = kv_ref.shape[0], kv_ref.shape[2], kv_ref.shape[3]
    tall = GROUP * rows
    row_of = lax.broadcasted_iota(jnp.int32, (tall, rows * count), 0) % rows
    col = lax.broadcasted_iota(jnp.int32, (tall, rows * count), 1)
    lengths = jnp.concatenate([len_ref[:, 0:1]] * GROUP, axis=0)
    live = (col // count == row_of) & (col % count < lengths)
    lane = lax.broadcasted_iota(jnp.int32, (rows, LANES), 1)
    lse_all = jnp.zeros((rows, LANES), jnp.float32)
    for g in range(kv_heads):
        heads = range(g * GROUP, (g + 1) * GROUP)
        q = jnp.concatenate([q_ref[:, h * HD : (h + 1) * HD] for h in heads], axis=0)
        keys = kv_ref[:, 0, g].reshape(rows * count, HD)
        values = kv_ref[:, 1, g].reshape(rows * count, HD)
        s = jnp.where(live, nt_dot(q, keys) * SCALE2, -jnp.inf)
        top = jnp.max(s, axis=1, keepdims=True)
        w = jnp.exp2(s - top)
        total = jnp.sum(w, axis=1, keepdims=True)
        part = nn_dot(w.astype(jnp.bfloat16), values) / total
        lse = top + jnp.log(total) * LOG2E
        for i, h in enumerate(heads):
            sum_ref[:, h * HD : (h + 1) * HD] = part[i * rows : (i + 1) * rows]
            lse_all = jnp.where(lane == h, lse[i * rows : (i + 1) * rows], lse_all)
    lse_ref[...] = lse_all


def suffix_attend(local_q, suffix_kv, lengths):
    rows_home, row_width = local_q.shape
    kv_heads, count = suffix_kv.shape[2], suffix_kv.shape[3]
    rows = math.gcd(rows_home, 16)
    wide_lengths = jnp.broadcast_to(lengths[:, None], (rows_home, LANES))
    return pl.pallas_call(
        suffix_kernel,
        grid=(rows_home // rows,),
        out_shape=(
            jax.ShapeDtypeStruct((rows_home, row_width), jnp.float32),
            jax.ShapeDtypeStruct((rows_home, LANES), jnp.float32),
        ),
        in_specs=[
            pl.BlockSpec((rows, row_width), lambda b: (b, 0)),
            pl.BlockSpec((rows, 2, kv_heads, count, HD), lambda b: (b, 0, 0, 0, 0)),
            pl.BlockSpec((rows, LANES), lambda b: (b, 0)),
        ],
        out_specs=(
            pl.BlockSpec((rows, row_width), lambda b: (b, 0)),
            pl.BlockSpec((rows, LANES), lambda b: (b, 0)),
        ),
        compiler_params=pltpu.CompilerParams(vmem_limit_bytes=40 << 20),
        cost_estimate=pl.CostEstimate(
            flops=4 * rows_home * row_width * count * rows,
            bytes_accessed=4 * rows_home * kv_heads * count * HD + 6 * rows_home * row_width,
            transcendentals=rows_home * row_width // HD * count * rows,
        ),
        name="suffix_attend",
    )(local_q, suffix_kv, wide_lengths)


def merge_kernel(pick_ref, back_ref, sum_ref, lse_ref, out_ref):
    row_width = out_ref.shape[1]
    heads = row_width // HD
    pick = pick_ref[...]
    prefix_lse = nn_dot(pick, back_ref[:, row_width : row_width + LANES])
    for i in range(1, 3):
        left = row_width + i * LANES
        prefix_lse = prefix_lse + nn_dot(pick, back_ref[:, left : left + LANES])
    suffix_lse = lse_ref[...]
    joint = jnp.maximum(prefix_lse, suffix_lse)
    prefix_mass = jnp.exp2(prefix_lse - joint)
    suffix_mass = jnp.exp2(suffix_lse - joint)
    mass = prefix_mass + suffix_mass
    prefix_share = prefix_mass / mass
    suffix_share = suffix_mass / mass
    for h in range(heads):
        cols = slice(h * HD, (h + 1) * HD)
        part = nn_dot(pick, back_ref[:, cols])
        mixed = prefix_share[:, h : h + 1] * part + suffix_share[:, h : h + 1] * sum_ref[:, cols]
        out_ref[:, cols] = mixed.astype(jnp.bfloat16)


def merge(pick, back, suffix_sum, suffix_lse):
    rows_home, row_width = suffix_sum.shape
    return pl.pallas_call(
        merge_kernel,
        out_shape=jax.ShapeDtypeStruct((rows_home, row_width), jnp.bfloat16),
        name="merge",
    )(pick, back, suffix_sum, suffix_lse)


def split_three(x):
    high = lax.reduce_precision(x, 8, 7)
    rest = x - high
    middle = lax.reduce_precision(rest, 8, 7)
    low = rest - middle
    return [piece.astype(jnp.bfloat16) for piece in (high, middle, low)]


def on_device(queries, suffix_kv, suffix_lengths, prefix_kv, tree_ids, owner_map):
    owners = lax.axis_size("prefix")
    local_q = lax.all_to_all(queries, "tensor", split_axis=1, concat_axis=0, tiled=True)
    rows_home, row_width = local_q.shape
    capacity = max(2, 2 * rows_home // owners)
    slots = owners * capacity
    prompts = owner_map.shape[0]
    prompt_iota = jnp.arange(prompts, dtype=jnp.int32)
    prompt_match = tree_ids[:, None] == prompt_iota[None, :]
    owner_row = jnp.sum(jnp.where(prompt_match, owner_map[None, :], 0), axis=1)
    row_iota = jnp.arange(rows_home, dtype=jnp.int32)
    earlier = (tree_ids[:, None] == tree_ids[None, :]) & (row_iota[None, :] < row_iota[:, None])
    slot_rank = jnp.sum(earlier.astype(jnp.int32), axis=1)
    slot_of = owner_row * capacity + slot_rank
    slot_iota = jnp.arange(slots, dtype=jnp.int32)
    pick = (slot_of[:, None] == slot_iota[None, :]).astype(jnp.bfloat16)
    outgoing = lax.dot_general(
        pick, local_q, (((0,), (0,)), ((), ())), preferred_element_type=jnp.float32
    ).astype(jnp.bfloat16)
    arrived = lax.all_to_all(
        outgoing.reshape(owners, capacity, row_width),
        "prefix",
        split_axis=0,
        concat_axis=0,
        tiled=True,
    ).reshape(slots, row_width)
    suffix_sum, suffix_lse = suffix_attend(local_q, suffix_kv, suffix_lengths)
    part, lse = prefix_attend(arrived, prefix_kv)
    packed = jnp.concatenate([part] + split_three(lse), axis=1)
    back = lax.all_to_all(
        packed.reshape(owners, capacity, packed.shape[1]),
        "prefix",
        split_axis=0,
        concat_axis=0,
        tiled=True,
    ).reshape(slots, packed.shape[1])
    attended = merge(pick, back, suffix_sum, suffix_lse)
    return lax.all_to_all(attended, "tensor", split_axis=0, concat_axis=1, tiled=True)


def solution(mesh):
    in_specs = (
        P(("prefix", "tensor"), None),
        P("prefix", None, "tensor", None, None),
        P("prefix"),
        P("prefix", None, "tensor", None, None),
        P("prefix"),
        P(),
    )
    out_specs = P(("prefix", "tensor"), None)
    return jax.shard_map(
        on_device, mesh=mesh, in_specs=in_specs, out_specs=out_specs, check_vma=False
    )
```

time: 202 us -> 133 us (0.66)
  the two profiles are of different devices: /device:TPU:10 before, /device:TPU:0 now
where the time goes in v1:
time: 133 us; the launch traced here: 132 us
  blocking collectives  43.4 us (33%)
  Pallas kernels  42.9 us (32%)
  waiting for transfers between devices  19.8 us (15%)
  local copies, waits for them, and re-layouts  12.1 us (9%)
  starting transfers between devices  9.29 us (7%)
  other arithmetic  3.46 us (3%)
    pallas_call x1, Pallas kernels, prefix_attend(): pl.pallas_call(prefix_kernel, grid=(kv_heads,), out_shape=(jax.ShapeDtype...  33.6 us
    all_to_all x1, blocking collectives, on_device(): lax.all_to_all(outgoing.reshape(owners, capacity, row_width), 'prefix', s...  30.6 us
    all_to_all x1, blocking collectives, on_device(): lax.all_to_all(attended, 'tensor', split_axis=0, concat_axis=1, tiled=True)  12.8 us
    all_to_all x1, waiting for transfers between devices, on_device(): lax.all_to_all(packed.reshape(owners, capacity, packed.shape[1]), 'prefix...  12.8 us
    unnamed x12, local copies, waits for them, and re-layouts  9.38 us
    all_to_all x1, waiting for transfers between devices, on_device(): lax.all_to_all(queries, 'tensor', split_axis=1, concat_axis=0, tiled=True)  7.04 us
    pallas_call x1, Pallas kernels, suffix_attend(): pl.pallas_call(suffix_kernel, grid=(rows_home // rows,), out_shape=(jax.S...  6 us
    all_to_all x1, starting transfers between devices, on_device(): lax.all_to_all(packed.reshape(owners, capacity, packed.shape[1]), 'prefix...  5.02 us
  transfers between devices with their start and end apart: 2, of which 2 were waited for; matrix products, arithmetic and copies ran while one was open for 2% of the time, Pallas kernels for 5%

profile of v1, /device:TPU:0, one launch (start us, length us, event | category | flops | bytes accessed | tf_op | source)
XLA Modules:
  0.0 131.6 jit_solution(11226952956034639899)
XLA Ops:
  0.0 1.9 %copy.14 = bf16[4,2,8,4096]{3,2,0,1:T(8,128)(2,1)} copy(bf16[4,2,8,4096]{3,2,1,0:T(8,128)(2,1)} %bitcast.24) | data formatting | bytes 1048576 | tf_op jit(solution)/shard_map/all_to_all | solution.py:196
  1.9 4.3 %all-to-all-start = ((bf16[32,2,4096]{2,0,1:T(8,128)(2,1)}), bf16[32,2,4096]{2,0,1:T(8,128)(2,1)S(1)}, u32[]{:S(2)}, u32[]{:S(2)}) async-start(bf16[32,2,4096]{2,0,1:T(8,128)(2,1)} %bitcast.17), calls=%async_computation | async-start | bytes 1048576 | tf_op jit(solution)/shard_map/all_to_all | solution.py:196
  6.1 0.9 convert_reduce_fusion
  7.0 0.8 select_reduce_fusion
  7.8 7.0 %all-to-all-done = bf16[32,2,4096]{2,0,1:T(8,128)(2,1)S(1)} async-done(((bf16[32,2,4096]{2,0,1:T(8,128)(2,1)}), bf16[32,2,4096]{2,0,1:T(8,128)(2,1)S(1)}, u32[]{:S(2)}, u32[]{:S(2)}) %all-to-all-start) | async-done | bytes 524320 | tf_op jit(solution)/shard_map/all_to_all | solution.py:196
  14.9 0.5 fusion
  15.4 30.6 %all_to_all.48 = bf16[16,8,4096]{2,1,0:T(8,128)(2,1)S(1)} all-to-all(bf16[16,8,4096]{2,1,0:T(8,128)(2,1)S(1)} %fusion), channel_id=1, replica_groups=mesh['prefix'=16,'tensor'=2] {'prefix'}, dimensions={0} | all-to-all | bytes 2097152 | tf_op jit(solution)/shard_map/all_to_all | solution.py:213
  46.0 0.0 copy-start.3
  46.0 3.4 %copy-done.3 = bf16[1,2,4,4096,128]{4,3,2,1,0:T(8,128)(2,1)S(1)} copy-done((bf16[1,2,4,4096,128]{4,3,2,1,0:T(8,128)(2,1)S(1)}, bf16[1,2,4,4096,128]{4,3,2,1,0:T(8,128)(2,1)}, u32[]{:S(2)}) %copy-start.3) | copy-done | bytes 8388632
  49.4 33.6 %prefix_attend.1 = (bf16[128,4096]{1,0:T(8,128)(2,1)S(1)}, f32[128,128]{1,0:T(8,128)S(1)}) custom-call(bf16[128,4096]{1,0:T(8,128)(2,1)S(1)} %bitcast.20, bf16[1,2,4,4096,128]{4,3,2,1,0:T(8,128)(2,1)S(1)} %copy-done.3), custom_call_target="tpu_custom_call" | custom-call | flops 8589934592 | bytes 10485760 | tf_op jit(solution)/shard_map/prefix_attend/pallas_call | solution.py:73
  83.1 0.0 copy-start.5
  83.1 1.1 maximum_bitcast_fusion
  84.2 5.0 %all-to-all-start.2 = ((bf16[16,8,4480]{2,1,0:T(8,128)(2,1)}), bf16[16,8,4480]{2,1,0:T(8,128)(2,1)S(1)}, u32[]{:S(2)}, u32[]{:S(2)}) async-start(bf16[16,8,4480]{2,1,0:T(8,128)(2,1)} %maximum_bitcast_fusion), calls=%async_computation.2 | async-start | bytes 2293760 | tf_op jit(solution)/shard_map/all_to_all | solution.py:223
  89.2 0.7 fusion.2.pick_ref
  89.9 0.0 copy-done.5
  89.9 0.1 broadcast_in_dim.16.len_ref
  89.9 0.0 copy-start
  89.9 3.4 %copy-done = bf16[64,2,4,64,128]{4,3,2,1,0:T(8,128)(2,1)S(1)} copy-done((bf16[64,2,4,64,128]{4,3,2,1,0:T(8,128)(2,1)S(1)}, bf16[64,2,4,64,128]{4,3,2,1,0:T(8,128)(2,1)}, u32[]{:S(2)}) %copy-start) | copy-done | bytes 8388632
  93.3 6.0 %suffix_attend.1 = (f32[64,4096]{1,0:T(8,128)S(1)}, f32[64,128]{1,0:T(8,128)S(1)}) custom-call(bf16[64,4096]{1,0:T(8,128)(2,1)S(1)} %bitcast.19, bf16[64,2,4,64,128]{4,3,2,1,0:T(8,128)(2,1)S(1)} %copy-done, s32[64,128]{1,0:T(8,128)S(1)} %broadcast_in_dim.16.len_ref), custom_call_target="tpu_custom_call" | custom-call | flops 1073741824 | bytes 9961472 | tf_op jit(solution)/shard_map/suffix_attend/pallas_call | solution.py:129
  99.3 0.0 copy-start.1
  99.3 1.0 copy-done.1
  100.3 0.0 copy-start.2
  100.3 0.6 copy-done.2
  100.9 12.8 %all-to-all-done.2 = bf16[16,8,4480]{2,1,0:T(8,128)(2,1)S(1)} async-done(((bf16[16,8,4480]{2,1,0:T(8,128)(2,1)}), bf16[16,8,4480]{2,1,0:T(8,128)(2,1)S(1)}, u32[]{:S(2)}, u32[]{:S(2)}) %all-to-all-start.2) | async-done | bytes 1146912 | tf_op jit(solution)/shard_map/all_to_all | solution.py:223
  113.7 0.0 copy-start.4
  113.7 1.0 copy-done.4
  114.7 3.3 %merge.1 = bf16[64,4096]{1,0:T(8,128)(2,1)} custom-call(bf16[64,128]{1,0:T(8,128)(2,1)} %fusion.2.pick_ref, bf16[128,4480]{1,0:T(8,128)(2,1)} %bitcast.21, f32[64,4096]{1,0:T(8,128)} %copy-done.1, f32[64,128]{1,0:T(8,128)} %copy-done.2), custom_call_target="tpu_custom_call" | custom-call | tf_op jit(solution)/shard_map/merge/pallas_call | solution.py:179
  118.0 12.8 %all_to_all.49 = bf16[2,32,4096]{2,1,0:T(8,128)(2,1)S(1)} all-to-all(bf16[2,32,4096]{2,1,0:T(8,128)(2,1)} %bitcast.23), channel_id=1, replica_groups=mesh['prefix'=16,'tensor'=2] {'tensor'}, dimensions={0} | all-to-all | bytes 1048576 | tf_op jit(solution)/shard_map/all_to_all | solution.py:231
  130.7 0.8 copy.12
  (2 shorter events, 0.0 us)
Async XLA Ops:
  1.9 13.0 %all-to-all-start = ((bf16[32,2,4096]{2,0,1:T(8,128)(2,1)}), bf16[32,2,4096]{2,0,1:T(8,128)(2,1)S(1)}, u32[]{:S(2)}, u32[]{:S(2)}) async-start(bf16[32,2,4096]{2,0,1:T(8,128)(2,1)} %bitcast.17), calls=%async_computation | async-start | bytes 1048576 | tf_op jit(solution)/shard_map/all_to_all | solution.py:196
  46.0 3.4 %copy-start.3 = (bf16[1,2,4,4096,128]{4,3,2,1,0:T(8,128)(2,1)S(1)}, bf16[1,2,4,4096,128]{4,3,2,1,0:T(8,128)(2,1)}, u32[]{:S(2)}) copy-start(bf16[1,2,4,4096,128]{4,3,2,1,0:T(8,128)(2,1)} %kv_ref.2) | copy-start | bytes 25165828
  83.1 6.8 %copy-start.5 = (s32[64]{0:T(128)S(1)}, s32[64]{0:T(128)}, u32[]{:S(2)}) copy-start(s32[64]{0:T(128)} %param.8) | copy-start | bytes 772
  84.2 29.5 %all-to-all-start.2 = ((bf16[16,8,4480]{2,1,0:T(8,128)(2,1)}), bf16[16,8,4480]{2,1,0:T(8,128)(2,1)S(1)}, u32[]{:S(2)}, u32[]{:S(2)}) async-start(bf16[16,8,4480]{2,1,0:T(8,128)(2,1)} %maximum_bitcast_fusion), calls=%async_computation.2 | async-start | bytes 2293760 | tf_op jit(solution)/shard_map/all_to_all | solution.py:223
  89.9 3.4 %copy-start = (bf16[64,2,4,64,128]{4,3,2,1,0:T(8,128)(2,1)S(1)}, bf16[64,2,4,64,128]{4,3,2,1,0:T(8,128)(2,1)}, u32[]{:S(2)}) copy-start(bf16[64,2,4,64,128]{4,3,2,1,0:T(8,128)(2,1)} %kv_ref.3) | copy-start | bytes 25165828
  99.3 1.0 copy-start.1
  100.3 0.6 copy-start.2
  113.7 1.0 copy-start.4

commit v2 on v0

v2 whole, which is shorter than its diff:
```python
import functools
import math

import jax
import jax.numpy as jnp
from jax import lax
from jax.experimental import pallas as pl
from jax.experimental.pallas import tpu as pltpu
from jax.sharding import PartitionSpec as P

H = 64
KVH = 8
HD = 128
LANES = 128
GROUP = H // KVH
LOG2E = 1.4426950408889634
SCALE2 = LOG2E / math.sqrt(HD)
MESH = pl.DeviceIdType.MESH


def nt_dot(a, b):
    return lax.dot_general(a, b, (((1,), (1,)), ((), ())), preferred_element_type=jnp.float32)


def nn_dot(a, b):
    return lax.dot_general(a, b, (((1,), (0,)), ((), ())), preferred_element_type=jnp.float32)


def lane_column(block, lane, index):
    return jnp.sum(jnp.where(lane == index, block, 0.0), axis=1, keepdims=True)


def attend_tile(q, kv_ref, g, chunk):
    length = kv_ref.shape[2]
    top = total = acc = None
    for start in range(0, length, chunk):
        s = nt_dot(q, kv_ref[0, g, start : start + chunk, :]) * SCALE2
        here = jnp.max(s, axis=1, keepdims=True)
        new_top = here if top is None else jnp.maximum(top, here)
        w = jnp.exp2(s - new_top)
        w_sum = jnp.sum(w, axis=1, keepdims=True)
        w_v = nn_dot(w.astype(jnp.bfloat16), kv_ref[1, g, start : start + chunk, :])
        if top is None:
            total, acc = w_sum, w_v
        else:
            fade = jnp.exp2(top - new_top)
            total = total * fade + w_sum
            acc = acc * fade + w_v
        top = new_top
    return acc / total, top + jnp.log(total) * LOG2E


def whole_kernel(
    owners, parts, q_ref, pick_ref, pick_t_ref, len_ref, suffix_hbm, prefix_hbm, out_ref,
    home, home_f, outgoing, arrived, returned, back, lse_out, lse_back, stage, stage_two,
    lse_stage, lse_home, share_p, share_s, suffix_sum, attended, suffix_v, prefix_v,
    bar_home_send, home_recv, out_send, out_recv, ret_send, ret_recv,
    lse_send, lse_recv, att_send, att_recv, own_sem, suffix_sem, prefix_sem,
):
    me = lax.axis_index("prefix")
    me_t = lax.axis_index("tensor")
    kv_heads, _, capacity, wide = outgoing.shape
    part_rows = home.shape[1]
    row_width = home.shape[2]
    rows_home = home_f.shape[0]
    slots = stage.shape[0]
    blocks = suffix_sem.shape[0]
    rows = rows_home // blocks
    count = suffix_v.shape[3]

    def peer(d):
        return lax.rem(me + d, owners)

    def peer_t(d):
        return lax.rem(me_t + d, parts)

    def suffix_copy(b):
        at = pl.ds(b * rows, rows)
        return pltpu.make_async_copy(suffix_hbm.at[at], suffix_v.at[at], suffix_sem.at[b])

    def prefix_copy(g):
        return pltpu.make_async_copy(
            prefix_hbm.at[0, :, g], prefix_v.at[:, g], prefix_sem.at[g]
        )

    for b in range(blocks):
        suffix_copy(b).start()
    for g in range(kv_heads):
        prefix_copy(g).start()

    barrier = pltpu.get_barrier_semaphore()

    def greet(d, carry):
        pl.semaphore_signal(barrier, inc=1, device_id={"prefix": peer(d)}, device_id_type=MESH)
        return carry

    def greet_t(d, carry):
        pl.semaphore_signal(barrier, inc=1, device_id={"tensor": peer_t(d)}, device_id_type=MESH)
        return carry

    lax.fori_loop(1, owners, greet, 0)
    lax.fori_loop(1, parts, greet_t, 0)
    pl.semaphore_wait(barrier, owners + parts - 2)

    def home_copy(d):
        cols = pl.ds(pl.multiple_of(peer_t(d) * row_width, LANES), row_width)
        return pltpu.make_async_remote_copy(
            src_ref=q_ref.at[:, cols], dst_ref=home.at[me_t],
            send_sem=bar_home_send.at[d], recv_sem=home_recv.at[d],
            device_id={"tensor": peer_t(d)}, device_id_type=MESH,
        )

    def exchange(src, dst, send_sem, recv_sem, d):
        return pltpu.make_async_remote_copy(
            src_ref=src, dst_ref=dst, send_sem=send_sem, recv_sem=recv_sem,
            device_id={"prefix": peer(d)}, device_id_type=MESH,
        )

    def out_copy(g, d):
        return exchange(
            outgoing.at[g, peer(d)], arrived.at[g, me], out_send.at[g, d], out_recv.at[g, d], d
        )

    def ret_copy(g, d):
        return exchange(
            returned.at[g, peer(d)], back.at[g, me], ret_send.at[g, d], ret_recv.at[g, d], d
        )

    def lse_copy(d):
        return exchange(lse_out.at[peer(d)], lse_back.at[me], lse_send.at[d], lse_recv.at[d], d)

    def att_copy(g, d):
        cols = pl.ds(pl.multiple_of(me_t * row_width + g * wide, LANES), wide)
        return pltpu.make_async_remote_copy(
            src_ref=attended.at[g, peer_t(d)], dst_ref=out_ref.at[:, cols],
            send_sem=att_send.at[g, d], recv_sem=att_recv.at[g, d],
            device_id={"tensor": peer_t(d)}, device_id_type=MESH,
        )

    def loop(low, high, act):
        def step(i, carry):
            act(i)
            return carry
        lax.fori_loop(low, high, step, 0)

    loop(1, parts, lambda d: home_copy(d).start())
    own_cols = pl.ds(pl.multiple_of(me_t * row_width, LANES), row_width)
    own_home = pltpu.make_async_copy(q_ref.at[:, own_cols], home.at[me_t], own_sem.at[0, 0])
    own_home.start()
    own_home.wait()
    loop(1, parts, lambda d: home_copy(d).wait_recv())
    for t in range(parts):
        home_f[t * part_rows : (t + 1) * part_rows, :] = home[t].astype(jnp.float32)

    def spread(target, g, source):
        for o in range(owners):
            target[g, o] = source[o * capacity : (o + 1) * capacity, :].astype(jnp.bfloat16)

    def gather(target, g, source):
        for o in range(owners):
            target[o * capacity : (o + 1) * capacity, :] = source[g, o].astype(jnp.float32)

    def wide_cols(g):
        return pl.ds(pl.multiple_of(g * wide, LANES), wide)

    def own_out(g):
        return pltpu.make_async_copy(outgoing.at[g, me], arrived.at[g, me], own_sem.at[1, g])

    def own_back(g):
        return pltpu.make_async_copy(returned.at[g, me], back.at[g, me], own_sem.at[2, g])

    def own_att(g):
        cols = pl.ds(pl.multiple_of(me_t * row_width + g * wide, LANES), wide)
        return pltpu.make_async_copy(attended.at[g, me_t], out_ref.at[:, cols], own_sem.at[3, g])

    def dispatch(g):
        stage[...] = nn_dot(pick_t_ref[...], home_f[:, wide_cols(g)].astype(jnp.bfloat16))
        spread(outgoing, g, stage)
        own_out(g).start()
        loop(1, owners, lambda d: out_copy(g, d).start())

    loop(0, kv_heads, dispatch)

    tall = GROUP * rows
    row_of = lax.broadcasted_iota(jnp.int32, (tall, rows * count), 0) % rows
    col = lax.broadcasted_iota(jnp.int32, (tall, rows * count), 1)
    own_block = col // count == row_of
    place = col % count
    row_lane = lax.broadcasted_iota(jnp.int32, (rows, LANES), 1)
    slot_lane = lax.broadcasted_iota(jnp.int32, (slots, LANES), 1)
    home_lane = lax.broadcasted_iota(jnp.int32, (rows_home, LANES), 1)
    lse_stage[...] = jnp.zeros_like(lse_stage)
    lse_home[...] = jnp.zeros_like(lse_home)

    def suffix_block(b):
        suffix_copy(b).wait()
        at = pl.ds(pl.multiple_of(b * rows, rows), rows)
        lengths = jnp.concatenate([len_ref[at, 0:1]] * GROUP, axis=0)
        live = own_block & (place < lengths)

        def suffix_head(g):
            cols = [
                pl.ds(pl.multiple_of((g * GROUP + i) * HD, HD), HD) for i in range(GROUP)
            ]
            q = jnp.concatenate([home_f[at, c] for c in cols], axis=0).astype(jnp.bfloat16)
            keys = suffix_v[at, 0, g].reshape(rows * count, HD)
            values = suffix_v[at, 1, g].reshape(rows * count, HD)
            s = jnp.where(live, nt_dot(q, keys) * SCALE2, -jnp.inf)
            top = jnp.max(s, axis=1, keepdims=True)
            w = jnp.exp2(s - top)
            total = jnp.sum(w, axis=1, keepdims=True)
            part = nn_dot(w.astype(jnp.bfloat16), values) / total
            lse = top + jnp.log(total) * LOG2E
            for i in range(GROUP):
                piece = slice(i * rows, (i + 1) * rows)
                suffix_sum[at, cols[i]] = part[piece]
                lse_home[at, :] = jnp.where(
                    row_lane == g * GROUP + i, lse[piece], lse_home[at, :]
                )

        loop(0, kv_heads, suffix_head)

    loop(0, blocks, suffix_block)

    pair = 2
    chunk = min(1024, prefix_v.shape[2])

    def prefix_head(g):
        own_out(g).wait()
        loop(1, owners, lambda d: out_copy(g, d).wait_recv())
        gather(stage, g, arrived)
        prefix_copy(g).wait()

        def tile(t):
            cols = [pl.ds(pl.multiple_of((t * pair + i) * HD, HD), HD) for i in range(pair)]
            q = jnp.concatenate([stage[:, c] for c in cols], axis=0).astype(jnp.bfloat16)
            part, lse = attend_tile(q, prefix_v, g, chunk)
            for i in range(pair):
                piece = slice(i * slots, (i + 1) * slots)
                stage_two[:, cols[i]] = part[piece]
                lse_stage[...] = jnp.where(
                    slot_lane == g * GROUP + t * pair + i, lse[piece], lse_stage[...]
                )

        loop(0, GROUP // pair, tile)
        spread(returned, g, stage_two)
        own_back(g).start()
        loop(1, owners, lambda d: ret_copy(g, d).start())

    loop(0, kv_heads, prefix_head)

    for o in range(owners):
        lse_out[o] = lse_stage[o * capacity : (o + 1) * capacity, :]
    own_lse = pltpu.make_async_copy(lse_out.at[me], lse_back.at[me], own_sem.at[0, 0])
    own_lse.start()
    loop(1, owners, lambda d: lse_copy(d).start())
    own_lse.wait()
    loop(1, owners, lambda d: lse_copy(d).wait_recv())
    for o in range(owners):
        lse_stage[o * capacity : (o + 1) * capacity, :] = lse_back[o]
    prefix_lse = lax.dot_general(
        pick_ref[...].astype(jnp.float32), lse_stage[...], (((1,), (0,)), ((), ())),
        precision=lax.Precision.HIGHEST, preferred_element_type=jnp.float32,
    )
    suffix_lse = lse_home[...]
    joint = jnp.maximum(prefix_lse, suffix_lse)
    prefix_mass = jnp.exp2(prefix_lse - joint)
    suffix_mass = jnp.exp2(suffix_lse - joint)
    mass = prefix_mass + suffix_mass
    share_p[...] = prefix_mass / mass
    share_s[...] = suffix_mass / mass

    def merge_head(g):
        own_back(g).wait()
        loop(1, owners, lambda d: ret_copy(g, d).wait_recv())
        gather(stage, g, back)
        picked = nn_dot(pick_ref[...], stage[...].astype(jnp.bfloat16))
        for i in range(GROUP):
            head = g * GROUP + i
            from_prefix = lane_column(share_p[...], home_lane, head)
            from_suffix = lane_column(share_s[...], home_lane, head)
            here = pl.ds(pl.multiple_of(head * HD, HD), HD)
            mixed = from_prefix * picked[:, i * HD : (i + 1) * HD]
            mixed = mixed + from_suffix * suffix_sum[:, here]
            for t in range(parts):
                attended[g, t, :, i * HD : (i + 1) * HD] = mixed[
                    t * part_rows : (t + 1) * part_rows
                ].astype(jnp.bfloat16)
        own_att(g).start()
        loop(1, parts, lambda d: att_copy(g, d).start())

    loop(0, kv_heads, merge_head)

    def finish(g):
        own_att(g).wait()
        loop(1, parts, lambda d: att_copy(g, d).wait())
        loop(1, owners, lambda d: out_copy(g, d).wait_send())
        loop(1, owners, lambda d: ret_copy(g, d).wait_send())

    loop(0, kv_heads, finish)
    loop(1, owners, lambda d: lse_copy(d).wait_send())
    loop(1, parts, lambda d: home_copy(d).wait_send())


def on_device(queries, suffix_kv, suffix_lengths, prefix_kv, tree_ids, owner_map):
    owners = lax.axis_size("prefix")
    parts = lax.axis_size("tensor")
    part_rows, full_width = queries.shape
    rows_home, row_width = part_rows * parts, full_width // parts
    kv_heads, count = suffix_kv.shape[2], suffix_kv.shape[3]
    length = prefix_kv.shape[3]
    wide = row_width // kv_heads
    capacity = max(2, 2 * rows_home // owners)
    slots = owners * capacity
    prompts = owner_map.shape[0]
    prompt_iota = jnp.arange(prompts, dtype=jnp.int32)
    prompt_match = tree_ids[:, None] == prompt_iota[None, :]
    owner_row = jnp.sum(jnp.where(prompt_match, owner_map[None, :], 0), axis=1)
    row_iota = jnp.arange(rows_home, dtype=jnp.int32)
    earlier = (tree_ids[:, None] == tree_ids[None, :]) & (row_iota[None, :] < row_iota[:, None])
    slot_rank = jnp.sum(earlier.astype(jnp.int32), axis=1)
    slot_of = owner_row * capacity + slot_rank
    slot_iota = jnp.arange(slots, dtype=jnp.int32)
    pick = (slot_of[:, None] == slot_iota[None, :]).astype(jnp.bfloat16)
    pick_t = (slot_of[None, :] == slot_iota[:, None]).astype(jnp.bfloat16)
    lengths = jnp.broadcast_to(suffix_lengths[:, None], (rows_home, LANES))
    blocks = rows_home // math.gcd(rows_home, 16)
    bf16, f32 = jnp.bfloat16, jnp.float32
    vmem = pl.BlockSpec(memory_space=pltpu.VMEM)
    hbm = pl.BlockSpec(memory_space=pl.ANY)
    dma = pltpu.SemaphoreType.DMA
    slot_block = (kv_heads, owners, capacity, wide)
    return pl.pallas_call(
        functools.partial(whole_kernel, owners, parts),
        out_shape=jax.ShapeDtypeStruct((part_rows, full_width), bf16),
        in_specs=[vmem, vmem, vmem, vmem, hbm, hbm],
        out_specs=vmem,
        scratch_shapes=[
            pltpu.VMEM((parts, part_rows, row_width), bf16),
            pltpu.VMEM((rows_home, row_width), f32),
            pltpu.VMEM(slot_block, bf16),
            pltpu.VMEM(slot_block, bf16),
            pltpu.VMEM(slot_block, bf16),
            pltpu.VMEM(slot_block, bf16),
            pltpu.VMEM((owners, capacity, LANES), f32),
            pltpu.VMEM((owners, capacity, LANES), f32),
            pltpu.VMEM((slots, wide), f32),
            pltpu.VMEM((slots, wide), f32),
            pltpu.VMEM((slots, LANES), f32),
            pltpu.VMEM((rows_home, LANES), f32),
            pltpu.VMEM((rows_home, LANES), f32),
            pltpu.VMEM((rows_home, LANES), f32),
            pltpu.VMEM((rows_home, row_width), f32),
            pltpu.VMEM((kv_heads, parts, part_rows, wide), bf16),
            pltpu.VMEM((rows_home, 2, kv_heads, count, HD), bf16),
            pltpu.VMEM((2, kv_heads, length, HD), bf16),
            dma((parts,)),
            dma((parts,)),
            dma((kv_heads, owners)),
            dma((kv_heads, owners)),
            dma((kv_heads, owners)),
            dma((kv_heads, owners)),
            dma((owners,)),
            dma((owners,)),
            dma((kv_heads, parts)),
            dma((kv_heads, parts)),
            dma((4, kv_heads)),
            dma((blocks,)),
            dma((kv_heads,)),
        ],
        compiler_params=pltpu.CompilerParams(
            collective_id=0, has_side_effects=True, vmem_limit_bytes=56 << 20
        ),
        name="whole_step",
    )(queries, pick, pick_t, lengths, suffix_kv, prefix_kv)


def solution(mesh):
    in_specs = (
        P(("prefix", "tensor"), None),
        P("prefix", None, "tensor", None, None),
        P("prefix"),
        P("prefix", None, "tensor", None, None),
        P("prefix"),
        P(),
    )
    out_specs = P(("prefix", "tensor"), None)
    return jax.shard_map(
        on_device, mesh=mesh, in_specs=in_specs, out_specs=out_specs, check_vma=False
    )
```

time: 202 us -> 85.7 us (0.42)
  the two profiles are of different devices: /device:TPU:10 before, /device:TPU:0 now
where the time goes in v2:
time: 85.7 us; the launch traced here: 85.5 us
  Pallas kernels  79.3 us (93%)
  local copies, waits for them, and re-layouts  3.2 us (4%)
  other arithmetic  2.98 us (3%)
    pallas_call x1, Pallas kernels, on_device(): pl.pallas_call(functools.partial(whole_kernel, owners, parts), out_shape=...  79.3 us
    unnamed x1, local copies, waits for them, and re-layouts  1.87 us

profile of v2, /device:TPU:0, one launch (start us, length us, event | category | flops | bytes accessed | tf_op | source)
XLA Modules:
  0.0 85.5 jit_solution(2439733540152601814)
XLA Ops:
  0.0 0.8 select_reduce_fusion
  0.8 0.9 %convert_reduce_fusion = s32[64]{0:T(128)S(1)} fusion(s32[64]{0:T(128)} %param.10), kind=kLoop, calls=%fused_computation.3 | loop fusion | flops 20416 | bytes 512 | tf_op jit(solution)/shard_map/reduce_sum | solution.py:321
  1.7 0.7 fusion.2.pick_ref
  2.4 0.6 fusion.pick_t_ref
  3.0 1.3 %broadcast_in_dim.16.len_ref = s32[64,128]{1,0:T(8,128)} broadcast(s32[64]{0:T(128)} %param.8), dimensions={0} | broadcast | bytes 33024 | tf_op jit(solution)/shard_map/broadcast_in_dim | solution.py:326
  4.3 79.3 %whole_step.1 = bf16[32,8192]{1,0:T(8,128)(2,1)} custom-call(bf16[32,8192]{1,0:T(8,128)(2,1)} %q_ref.1, bf16[64,128]{1,0:T(8,128)(2,1)} %fusion.2.pick_ref, bf16[128,64]{1,0:T(8,128)(2,1)} %fusion.pick_t_ref, s32[64,128]{1,0:T(8,128)} %broadcast_in_dim.16.len_ref, bf16[64,2,4,64,128]{4,3,2,1,0:T(8,128)(2,1)} %suffix_hbm.1, ...), custom_call_target="tpu_custom_call" | custom-call | tf_op jit(solution)/shard_map/whole_step/pallas_call | solution.py:333
  83.6 1.9 %copy.8 = bf16[32,8192]{1,0:T(8,128)(2,1)} copy(bf16[32,8192]{1,0:T(8,128)(2,1)} %whole_step.1) | data formatting | bytes 1048576
  (1 shorter events, 0.0 us)

commit v3 on v2

--- a/solution.py
+++ b/solution.py
@@ -51,17 +51,18 @@
 
 
 def whole_kernel(
-    owners, parts, q_ref, pick_ref, pick_t_ref, len_ref, suffix_hbm, prefix_hbm, out_ref,
-    home, home_f, outgoing, arrived, returned, back, lse_out, lse_back, stage, stage_two,
-    lse_stage, lse_home, share_p, share_s, suffix_sum, attended, suffix_v, prefix_v,
+    owners, parts, q_ref, tree_ref, len_ref, map_ref, suffix_hbm, prefix_hbm, out_ref,
+    pick_ref, pick_t_ref, home, home_f, outgoing, arrived, returned, back, lse_out, lse_back, stage, stage_two,
+    lse_stage, lse_in, lse_home, share_p, share_s, suffix_sum, attended, suffix_v, prefix_v,
+    len_all,
     bar_home_send, home_recv, out_send, out_recv, ret_send, ret_recv,
     lse_send, lse_recv, att_send, att_recv, own_sem, suffix_sem, prefix_sem,
 ):
     me = lax.axis_index("prefix")
     me_t = lax.axis_index("tensor")
     kv_heads, _, capacity, wide = outgoing.shape
-    part_rows = home.shape[1]
-    row_width = home.shape[2]
+    part_rows = home.shape[2]
+    row_width = home_f.shape[1]
     rows_home = home_f.shape[0]
     slots = stage.shape[0]
     blocks = suffix_sem.shape[0]
@@ -102,11 +103,11 @@
     lax.fori_loop(1, parts, greet_t, 0)
     pl.semaphore_wait(barrier, owners + parts - 2)
 
-    def home_copy(d):
-        cols = pl.ds(pl.multiple_of(peer_t(d) * row_width, LANES), row_width)
+    def home_copy(g, d):
+        cols = pl.ds(pl.multiple_of(peer_t(d) * row_width + g * wide, LANES), wide)
         return pltpu.make_async_remote_copy(
-            src_ref=q_ref.at[:, cols], dst_ref=home.at[me_t],
-            send_sem=bar_home_send.at[d], recv_sem=home_recv.at[d],
+            src_ref=q_ref.at[:, cols], dst_ref=home.at[g, me_t],
+            send_sem=bar_home_send.at[g, d], recv_sem=home_recv.at[g, d],
             device_id={"tensor": peer_t(d)}, device_id_type=MESH,
         )
 
@@ -126,8 +127,13 @@
             returned.at[g, peer(d)], back.at[g, me], ret_send.at[g, d], ret_recv.at[g, d], d
         )
 
-    def lse_copy(d):
-        return exchange(lse_out.at[peer(d)], lse_back.at[me], lse_send.at[d], lse_recv.at[d], d)
+    def lse_copy(g, d):
+        return exchange(
+            lse_out.at[g, peer(d)], lse_back.at[g, me], lse_send.at[g, d], lse_recv.at[g, d], d
+        )
+
+    def own_lse(g):
+        return pltpu.make_async_copy(lse_out.at[g, me], lse_back.at[g, me], own_sem.at[4, g])
 
     def att_copy(g, d):
         cols = pl.ds(pl.multiple_of(me_t * row_width + g * wide, LANES), wide)
@@ -143,14 +149,42 @@
             return carry
         lax.fori_loop(low, high, step, 0)
 
-    loop(1, parts, lambda d: home_copy(d).start())
-    own_cols = pl.ds(pl.multiple_of(me_t * row_width, LANES), row_width)
-    own_home = pltpu.make_async_copy(q_ref.at[:, own_cols], home.at[me_t], own_sem.at[0, 0])
-    own_home.start()
-    own_home.wait()
-    loop(1, parts, lambda d: home_copy(d).wait_recv())
-    for t in range(parts):
-        home_f[t * part_rows : (t + 1) * part_rows, :] = home[t].astype(jnp.float32)
+    def own_home(g):
+        cols = pl.ds(pl.multiple_of(me_t * row_width + g * wide, LANES), wide)
+        return pltpu.make_async_copy(q_ref.at[:, cols], home.at[g, me_t], own_sem.at[0, g])
+
+    def start_home(g):
+        loop(1, parts, lambda d: home_copy(g, d).start())
+        own_home(g).start()
+
+    loop(0, kv_heads, start_home)
+
+    f32 = jnp.float32
+    prompts = map_ref.shape[1]
+    row_at = lax.broadcasted_iota(jnp.int32, (rows_home, rows_home), 0)
+    col_at = lax.broadcasted_iota(jnp.int32, (rows_home, rows_home), 1)
+    on_diagonal = row_at == col_at
+
+    def as_column(row_vector):
+        spread_rows = jnp.broadcast_to(row_vector, (rows_home, rows_home))
+        return jnp.sum(jnp.where(on_diagonal, spread_rows, 0.0), axis=1, keepdims=True)
+
+    tree_row = tree_ref[...].astype(f32)
+    tree_col = as_column(tree_row)
+    len_col = as_column(len_ref[...].astype(f32)).astype(jnp.int32)
+    earlier = (tree_col == tree_row) & (col_at < row_at)
+    rank = jnp.sum(jnp.where(earlier, 1.0, 0.0), axis=1, keepdims=True)
+    prompt_at = lax.broadcasted_iota(jnp.int32, (rows_home, prompts), 1).astype(f32)
+    owner_of = jnp.sum(
+        jnp.where(prompt_at == tree_col, map_ref[...].astype(f32), 0.0), axis=1, keepdims=True
+    )
+    slot_of = owner_of * capacity + rank
+    slot_at = lax.broadcasted_iota(jnp.int32, (rows_home, slots), 1).astype(f32)
+    pick = jnp.where(slot_of == slot_at, 1.0, 0.0)
+    pick_ref[...] = pick.astype(jnp.bfloat16)
+    pick_t_ref[...] = pick.T.astype(jnp.bfloat16)
+    len_wide = jnp.broadcast_to(len_col, (rows_home, LANES))
+    len_all[...] = len_wide
 
     def spread(target, g, source):
         for o in range(owners):
@@ -174,6 +208,10 @@
         return pltpu.make_async_copy(attended.at[g, me_t], out_ref.at[:, cols], own_sem.at[3, g])
 
     def dispatch(g):
+        own_home(g).wait()
+        loop(1, parts, lambda d: home_copy(g, d).wait_recv())
+        for t in range(parts):
+            home_f[t * part_rows : (t + 1) * part_rows, wide_cols(g)] = home[g, t].astype(f32)
         stage[...] = nn_dot(pick_t_ref[...], home_f[:, wide_cols(g)].astype(jnp.bfloat16))
         spread(outgoing, g, stage)
         own_out(g).start()
@@ -195,7 +233,7 @@
     def suffix_block(b):
         suffix_copy(b).wait()
         at = pl.ds(pl.multiple_of(b * rows, rows), rows)
-        lengths = jnp.concatenate([len_ref[at, 0:1]] * GROUP, axis=0)
+        lengths = jnp.concatenate([len_all[at, 0:1]] * GROUP, axis=0)
         live = own_block & (place < lengths)
 
         def suffix_head(g):
@@ -222,7 +260,7 @@
 
     loop(0, blocks, suffix_block)
 
-    pair = 2
+    pair = 4
     chunk = min(1024, prefix_v.shape[2])
 
     def prefix_head(g):
@@ -243,34 +281,30 @@
                 )
 
         loop(0, GROUP // pair, tile)
+        for o in range(owners):
+            lse_out[g, o] = lse_stage[o * capacity : (o + 1) * capacity, :]
+        own_lse(g).start()
+        loop(1, owners, lambda d: lse_copy(g, d).start())
         spread(returned, g, stage_two)
         own_back(g).start()
         loop(1, owners, lambda d: ret_copy(g, d).start())
 
-    loop(0, kv_heads, prefix_head)
-
-    for o in range(owners):
-        lse_out[o] = lse_stage[o * capacity : (o + 1) * capacity, :]
-    own_lse = pltpu.make_async_copy(lse_out.at[me], lse_back.at[me], own_sem.at[0, 0])
-    own_lse.start()
-    loop(1, owners, lambda d: lse_copy(d).start())
-    own_lse.wait()
-    loop(1, owners, lambda d: lse_copy(d).wait_recv())
-    for o in range(owners):
-        lse_stage[o * capacity : (o + 1) * capacity, :] = lse_back[o]
-    prefix_lse = lax.dot_general(
-        pick_ref[...].astype(jnp.float32), lse_stage[...], (((1,), (0,)), ((), ())),
-        precision=lax.Precision.HIGHEST, preferred_element_type=jnp.float32,
-    )
-    suffix_lse = lse_home[...]
-    joint = jnp.maximum(prefix_lse, suffix_lse)
-    prefix_mass = jnp.exp2(prefix_lse - joint)
-    suffix_mass = jnp.exp2(suffix_lse - joint)
-    mass = prefix_mass + suffix_mass
-    share_p[...] = prefix_mass / mass
-    share_s[...] = suffix_mass / mass
-
     def merge_head(g):
+        own_lse(g).wait()
+        loop(1, owners, lambda d: lse_copy(g, d).wait_recv())
+        for o in range(owners):
+            lse_in[o * capacity : (o + 1) * capacity, :] = lse_back[g, o]
+        prefix_lse = lax.dot_general(
+            pick_ref[...].astype(f32), lse_in[...], (((1,), (0,)), ((), ())),
+            precision=lax.Precision.HIGHEST, preferred_element_type=f32,
+        )
+        suffix_lse = lse_home[...]
+        joint = jnp.maximum(prefix_lse, suffix_lse)
+        prefix_mass = jnp.exp2(prefix_lse - joint)
+        suffix_mass = jnp.exp2(suffix_lse - joint)
+        mass = prefix_mass + suffix_mass
+        share_p[...] = prefix_mass / mass
+        share_s[...] = suffix_mass / mass
         own_back(g).wait()
         loop(1, owners, lambda d: ret_copy(g, d).wait_recv())
         gather(stage, g, back)
@@ -289,17 +323,23 @@
         own_att(g).start()
         loop(1, parts, lambda d: att_copy(g, d).start())
 
-    loop(0, kv_heads, merge_head)
+    def head_step(g):
+        prefix_head(g)
+        merge_head(g - 1)
+
+    prefix_head(0)
+    loop(1, kv_heads, head_step)
+    merge_head(kv_heads - 1)
 
     def finish(g):
         own_att(g).wait()
         loop(1, parts, lambda d: att_copy(g, d).wait())
         loop(1, owners, lambda d: out_copy(g, d).wait_send())
         loop(1, owners, lambda d: ret_copy(g, d).wait_send())
+        loop(1, owners, lambda d: lse_copy(g, d).wait_send())
+        loop(1, parts, lambda d: home_copy(g, d).wait_send())
 
     loop(0, kv_heads, finish)
-    loop(1, owners, lambda d: lse_copy(d).wait_send())
-    loop(1, parts, lambda d: home_copy(d).wait_send())
 
 
 def on_device(queries, suffix_kv, suffix_lengths, prefix_kv, tree_ids, owner_map):
@@ -313,17 +353,6 @@
     capacity = max(2, 2 * rows_home // owners)
     slots = owners * capacity
     prompts = owner_map.shape[0]
-    prompt_iota = jnp.arange(prompts, dtype=jnp.int32)
-    prompt_match = tree_ids[:, None] == prompt_iota[None, :]
-    owner_row = jnp.sum(jnp.where(prompt_match, owner_map[None, :], 0), axis=1)
-    row_iota = jnp.arange(rows_home, dtype=jnp.int32)
-    earlier = (tree_ids[:, None] == tree_ids[None, :]) & (row_iota[None, :] < row_iota[:, None])
-    slot_rank = jnp.sum(earlier.astype(jnp.int32), axis=1)
-    slot_of = owner_row * capacity + slot_rank
-    slot_iota = jnp.arange(slots, dtype=jnp.int32)
-    pick = (slot_of[:, None] == slot_iota[None, :]).astype(jnp.bfloat16)
-    pick_t = (slot_of[None, :] == slot_iota[:, None]).astype(jnp.bfloat16)
-    lengths = jnp.broadcast_to(suffix_lengths[:, None], (rows_home, LANES))
     blocks = rows_home // math.gcd(rows_home, 16)
     bf16, f32 = jnp.bfloat16, jnp.float32
     vmem = pl.BlockSpec(memory_space=pltpu.VMEM)
@@ -336,16 +365,19 @@
         in_specs=[vmem, vmem, vmem, vmem, hbm, hbm],
         out_specs=vmem,
         scratch_shapes=[
-            pltpu.VMEM((parts, part_rows, row_width), bf16),
+            pltpu.VMEM((rows_home, slots), bf16),
+            pltpu.VMEM((slots, rows_home), bf16),
+            pltpu.VMEM((kv_heads, parts, part_rows, wide), bf16),
             pltpu.VMEM((rows_home, row_width), f32),
             pltpu.VMEM(slot_block, bf16),
             pltpu.VMEM(slot_block, bf16),
             pltpu.VMEM(slot_block, bf16),
             pltpu.VMEM(slot_block, bf16),
-            pltpu.VMEM((owners, capacity, LANES), f32),
-            pltpu.VMEM((owners, capacity, LANES), f32),
+            pltpu.VMEM((kv_heads, owners, capacity, LANES), f32),
+            pltpu.VMEM((kv_heads, owners, capacity, LANES), f32),
             pltpu.VMEM((slots, wide), f32),
             pltpu.VMEM((slots, wide), f32),
+            pltpu.VMEM((slots, LANES), f32),
             pltpu.VMEM((slots, LANES), f32),
             pltpu.VMEM((rows_home, LANES), f32),
             pltpu.VMEM((rows_home, LANES), f32),
@@ -354,17 +386,18 @@
             pltpu.VMEM((kv_heads, parts, part_rows, wide), bf16),
             pltpu.VMEM((rows_home, 2, kv_heads, count, HD), bf16),
             pltpu.VMEM((2, kv_heads, length, HD), bf16),
-            dma((parts,)),
-            dma((parts,)),
-            dma((kv_heads, owners)),
-            dma((kv_heads, owners)),
-            dma((kv_heads, owners)),
-            dma((kv_heads, owners)),
-            dma((owners,)),
-            dma((owners,)),
+            pltpu.VMEM((rows_home, LANES), jnp.int32),
             dma((kv_heads, parts)),
             dma((kv_heads, parts)),
-            dma((4, kv_heads)),
+            dma((kv_heads, owners)),
+            dma((kv_heads, owners)),
+            dma((kv_heads, owners)),
+            dma((kv_heads, owners)),
+            dma((kv_heads, owners)),
+            dma((kv_heads, owners)),
+            dma((kv_heads, parts)),
+            dma((kv_heads, parts)),
+            dma((5, kv_heads)),
             dma((blocks,)),
             dma((kv_heads,)),
         ],
@@ -372,7 +405,14 @@
             collective_id=0, has_side_effects=True, vmem_limit_bytes=56 << 20
         ),
         name="whole_step",
-    )(queries, pick, pick_t, lengths, suffix_kv, prefix_kv)
+    )(
+        queries,
+        tree_ids.reshape(1, rows_home),
+        suffix_lengths.reshape(1, rows_home),
+        owner_map.reshape(1, prompts),
+        suffix_kv,
+        prefix_kv,
+    )
 
 
 def solution(mesh):

time: 85.7 us -> 77.8 us (0.908)
  Pallas kernels: 79.3 us -> 75.8 us
  other arithmetic: 2.98 us -> 0 us
  local copies, waits for them, and re-layouts: 3.2 us -> 1.87 us
    pallas_call x1, Pallas kernels: 79.3 us -> 75.8 us  [on_device(): pl.pallas_call(functools.partial(whole_kernel, owners, parts), out_shape=...]
    reduce_sum x2 -> x0, other arithmetic: 1.66 us -> none  [the longest x1 0.91 us: on_device(): slot_rank = jnp.sum(earlier.astype(jnp.int32), axis=1)]
    broadcast_in_dim x1 -> x0, local copies, waits for them, and re-layouts: 1.33 us -> none  [on_device(): lengths = jnp.broadcast_to(suffix_lengths[:, None], (rows_home, LANES))]
    convert_element_type x2 -> x0, other arithmetic: 1.32 us -> none  [the longest x1 0.69 us: on_device(): pick = (slot_of[:, None] == slot_iota[None, :]).astype(jnp.bfloat16)]
where the time goes in v3:
time: 77.8 us; the launch traced here: 77.6 us
  Pallas kernels  75.8 us (97%)
  local copies, waits for them, and re-layouts  1.87 us (2%)
    pallas_call x1, Pallas kernels, on_device(): pl.pallas_call(functools.partial(whole_kernel, owners, parts), out_shape=...  75.8 us
    unnamed x1, local copies, waits for them, and re-layouts  1.87 us

profile of v3, /device:TPU:0, one launch (start us, length us, event | category | flops | bytes accessed | tf_op | source)
XLA Modules:
  0.0 77.6 jit_solution(9017840132733215014)
XLA Ops:
  0.0 75.8 %whole_step.1 = bf16[32,8192]{1,0:T(8,128)(2,1)} custom-call(bf16[32,8192]{1,0:T(8,128)(2,1)} %q_ref.1, s32[1,64]{1,0:T(1,128)} %bitcast.3, s32[1,64]{1,0:T(1,128)} %bitcast.4, s32[1,16]{1,0:T(1,128)} %bitcast.5, bf16[64,2,4,64,128]{4,3,2,1,0:T(8,128)(2,1)} %suffix_hbm.1, bf16[1,2,4,4096,128]{4,3,2,1,0:T(8,128)(2,1)} %prefix_hbm.1), custom_call_target="tpu_custom_call" | custom-call | tf_op jit(solution)/shard_map/whole_step/pallas_call | solution.py:362
  75.8 1.9 %copy.8 = bf16[32,8192]{1,0:T(8,128)(2,1)} copy(bf16[32,8192]{1,0:T(8,128)(2,1)} %whole_step.1) | data formatting | bytes 1048576
